TPU v7x, 128 devices: a whole 4x4x4 slice. The times are simulated.
128 devices in a mesh: sample: 16 (over y, x), col: 8 (over z, core).
Axes of the slice: x: 4, y: 4, z: 4, core: 2. Of those that a mesh axis runs over, the one named last changes fastest.
Arguments:
- block_inputs: bfloat16 [2048, 17, 17, 768], P(('sample', 'col')), may hold values from 0 to 100, as said below
- first_entry: bfloat16 [1, 1, 768, 384], replicated, may hold values from -0.3125 to 0.3125
- first_wide: bfloat16 [3, 3, 192, 320], replicated, may hold values from -0.21875 to 0.21875
- first_row: bfloat16 [1, 7, 192, 192], replicated, may hold values from -0.25 to 0.25
- first_column: bfloat16 [7, 1, 192, 192], replicated, may hold values from -0.25 to 0.25
- first_reduce: bfloat16 [3, 3, 192, 192], replicated, may hold values from -0.21875 to 0.21875
- second_entry: bfloat16 [1, 1, 1280, 1152], replicated, may hold values from -0.25 to 0.25
- second_row: bfloat16 [1, 3, 384, 384], replicated, may hold values from -0.25 to 0.25
- second_column: bfloat16 [3, 1, 384, 384], replicated, may hold values from -0.25 to 0.25
- second_deep: bfloat16 [3, 3, 448, 384], replicated, may hold values from -0.125 to 0.125
- deep_row: bfloat16 [1, 3, 384, 384], replicated, may hold values from -0.25 to 0.25
- deep_column: bfloat16 [3, 1, 384, 384], replicated, may hold values from -0.25 to 0.25
- pool_project: bfloat16 [1, 1, 1280, 192], replicated, may hold values from -0.25 to 0.25
Outputs:
- feature_mean: float32 [2048], replicated
- covariance: float32 [2048, 2048], P('sample', 'col')
Inputs may be any that keep to these rules, and one draw needn't show every extreme that they name: `block_inputs`: nonnegative activations.
All inputs are finite; a program needn't handle non-finite values.
Results may differ from a plain program's by a relative error of at most 0.0003.
Values sent between devices are 32-bit elements; how exact they have to be, the bound alone decides.
No kernel may reach another device: no remote copies, remote signals or barrier semaphores. Data moves between devices by JAX's collectives and lax.ppermute only.
A program may use at most 128 MiB of HBM per device.

v0:
```python
import jax
import jax.numpy as jnp
from jax import lax
from jax.sharding import PartitionSpec as P


def combined_all(part, axis, combine):
    gathered = jax.tree.map(lambda a: lax.all_gather(a, axis), part)

    def take(source):
        return jax.tree.map(lambda a: lax.dynamic_index_in_dim(a, source, 0, False), gathered)

    return lax.fori_loop(
        1, lax.axis_size(axis), lambda source, state: combine(state, take(source)), take(0)
    )


def rectify(inputs, kernel, stride, padding):
    result = lax.conv_general_dilated(
        inputs,
        kernel,
        (stride, stride),
        padding,
        dimension_numbers=("NHWC", "HWIO", "NHWC"),
        preferred_element_type=jnp.float32,
    )
    return jnp.maximum(result, 0.0).astype(jnp.bfloat16)


def spatial_mean(inputs):
    return jnp.mean(inputs.astype(jnp.float32), axis=(1, 2))


def network(
    block_inputs,
    first_entry,
    first_wide,
    first_row,
    first_column,
    first_reduce,
    second_entry,
    second_row,
    second_column,
    second_deep,
    deep_row,
    deep_column,
    pool_project,
):
    no_margin = ((0, 0), (0, 0))
    entry_out = rectify(block_inputs, first_entry, 1, no_margin)
    half_width = first_wide.shape[2]
    wide_out = rectify(entry_out[..., :half_width], first_wide, 2, no_margin)
    tower_out = rectify(entry_out[..., half_width:], first_row, 1, ((0, 0), (3, 3)))
    tower_out = rectify(tower_out, first_column, 1, ((3, 3), (0, 0)))
    tower_out = rectify(tower_out, first_reduce, 2, no_margin)
    maximum = lax.reduce_window(
        block_inputs,
        jnp.array(-jnp.inf, block_inputs.dtype),
        lax.max,
        (1, 3, 3, 1),
        (1, 2, 2, 1),
        "VALID",
    )
    middle = jnp.concatenate([wide_out, tower_out, maximum], axis=3)
    second = rectify(middle, second_entry, 1, no_margin)
    branch_width = second_row.shape[2]
    deep_width = second_deep.shape[2]
    plain_width = second_entry.shape[3] - branch_width - deep_width
    plain_out = second[..., :plain_width]
    branch_in = second[..., plain_width : plain_width + branch_width]
    deep_in = second[..., plain_width + branch_width :]
    row_a = rectify(branch_in, second_row, 1, ((0, 0), (1, 1)))
    col_a = rectify(branch_in, second_column, 1, ((1, 1), (0, 0)))
    deep_out = rectify(deep_in, second_deep, 1, ((1, 1), (1, 1)))
    row_b = rectify(deep_out, deep_row, 1, ((0, 0), (1, 1)))
    col_b = rectify(deep_out, deep_column, 1, ((1, 1), (0, 0)))
    pool_pad = ((0, 0), (1, 1), (1, 1), (0, 0))
    summed = lax.reduce_window(
        middle.astype(jnp.float32),
        jnp.array(0.0, jnp.float32),
        lax.add,
        (1, 3, 3, 1),
        (1, 1, 1, 1),
        pool_pad,
    )
    ones_map = jnp.ones((1, middle.shape[1], middle.shape[2], 1), jnp.float32)
    cell_count = lax.reduce_window(
        ones_map, jnp.array(0.0, jnp.float32), lax.add, (1, 3, 3, 1), (1, 1, 1, 1), pool_pad
    )
    averaged = (summed / cell_count).astype(jnp.bfloat16)
    pooled = rectify(averaged, pool_project, 1, no_margin)
    return jnp.concatenate(
        [
            spatial_mean(plain_out),
            spatial_mean(row_a),
            spatial_mean(col_a),
            spatial_mean(row_b),
            spatial_mean(col_b),
            spatial_mean(pooled),
        ],
        axis=1,
    )


def local(
    block_inputs,
    first_entry,
    first_wide,
    first_row,
    first_column,
    first_reduce,
    second_entry,
    second_row,
    second_column,
    second_deep,
    deep_row,
    deep_column,
    pool_project,
):
    features = network(
        block_inputs,
        first_entry,
        first_wide,
        first_row,
        first_column,
        first_reduce,
        second_entry,
        second_row,
        second_column,
        second_deep,
        deep_row,
        deep_column,
        pool_project,
    )
    gathered = lax.all_gather(features, "col", axis=0, tiled=True)
    width = gathered.shape[1]
    col_width = width // lax.axis_size("col")
    col_start = lax.axis_index("col") * col_width
    row_width = width // lax.axis_size("sample")
    row_start = lax.axis_index("sample") * row_width
    group_images = gathered.shape[0]
    total_images = group_images * lax.axis_size("sample")
    highest = lax.Precision.HIGHEST
    group_mean = jnp.sum(gathered, axis=0) / group_images
    centered = gathered - group_mean
    columns = lax.dynamic_slice_in_dim(centered, col_start, col_width, 1)
    moments = jnp.einsum(
        "nf,nc->fc", centered, columns, precision=highest, preferred_element_type=jnp.float32
    )
    members = jnp.array(group_images, jnp.float32)

    def combine(earlier, latter):
        count_a, mean_a, moment_a = earlier
        count_b, mean_b, moment_b = latter
        count_all = count_a + count_b
        mean_gap = mean_b - mean_a
        gap_columns = lax.dynamic_slice_in_dim(mean_gap, col_start, col_width, 0)
        mean_all = mean_a + mean_gap * (count_b / count_all)
        moment_all = (
            moment_a + moment_b + jnp.outer(mean_gap, gap_columns) * (count_a * count_b / count_all)
        )
        return (count_all, mean_all, moment_all)

    merged_count, feature_mean, merged_moments = combined_all(
        (members, group_mean, moments), "sample", combine
    )
    covariance = lax.dynamic_slice_in_dim(merged_moments, row_start, row_width, 0) / (
        total_images - 1
    )
    return (feature_mean, covariance)


def solution(mesh):
    placed = (
        P(("sample", "col"), None, None, None),
        P(),
        P(),
        P(),
        P(),
        P(),
        P(),
        P(),
        P(),
        P(),
        P(),
        P(),
        P(),
    )
    return jax.shard_map(
        local, mesh=mesh, in_specs=placed, out_specs=(P(), P("sample", "col")), check_vma=False
    )
```

profile of v0, /device:TPU:1, one launch (start us, length us, event | category | flops | bytes accessed | tf_op | source)
XLA Modules:
  0.0 411.1 jit_solution(14171061432312267951)
XLA Ops:
  7.2 5.7 %fusion.26 = bf16[16,8,8,768]{3,0,2,1:T(8,128)(2,1)} fusion(bf16[16,17,17,768]{3,0,2,1:T(8,128)(2,1)} %param.15), kind=kOutput, calls=%fused_computation.51 | output fusion | flops 6291456 | bytes 8675328 | tf_op jit(solution)/shard_map/reduce_window | solution.py:56
  12.9 4.1 maximum_convert_fusion
  17.1 3.0 maximum_convert_fusion.11
  20.1 11.7 %fusion.7 = bf16[16,17,17,192]{3,0,2,1:T(8,128)(2,1)} fusion(bf16[1,7,192,192]{3,2,1,0:T(8,128)(2,1)S(1)} %copy-done.10, bf16[16,17,17,384]{3,0,2,1:T(8,128)(2,1)S(1)} %maximum_convert_fusion), kind=kOutput, calls=%fused_computation.13 | convolution fusion | flops 2145779712 | bytes 4831232 | tf_op jit(solution)/shard_map/conv_general_dilated | solution.py:19
  31.7 9.4 %fusion.14 = bf16[16,8,8,192]{3,0,2,1:T(8,128)(2,1)} fusion(bf16[3,3,192,192]{3,2,1,0:T(8,128)(2,1)} %param.20, bf16[7,1,192,192]{3,2,1,0:T(8,128)(2,1)} %param.19, bf16[16,17,17,192]{3,0,2,1:T(8,128)(2,1)} %fusion.7), kind=kOutput, calls=%fused_computation.31 | convolution fusion | flops 2830089216 | bytes 3348480 | tf_op jit(solution)/shard_map/conv_general_dilated | solution.py:19
  41.1 5.4 %concatenate.6 = bf16[16,8,8,1280]{3,0,2,1:T(8,128)(2,1)} concatenate(bf16[16,8,8,320]{3,0,2,1:T(8,128)(2,1)} %maximum_convert_fusion.11, bf16[16,8,8,192]{3,0,2,1:T(8,128)(2,1)} %fusion.14, bf16[16,8,8,768]{3,0,2,1:T(8,128)(2,1)} %fusion.26), dimensions={3} | concatenate | bytes 5242880 | tf_op jit(solution)/shard_map/concatenate | solution.py:64
  46.5 6.3 %fusion.5 = bf16[16,8,8,1152]{3,0,2,1:T(8,128)(2,1)S(1)} fusion(bf16[16,8,8,1280]{3,0,2,1:T(8,128)(2,1)} %concatenate.6, bf16[1,1,1280,1152]{3,2,1,0:T(8,128)(2,1)} %param.21), kind=kOutput, calls=%fused_computation.11 | convolution fusion | flops 3022258176 | bytes 7929856 | tf_op jit(solution)/shard_map/conv_general_dilated | solution.py:19
  52.9 1.6 multiply_convert_fusion
  54.5 0.9 fusion.17
  55.6 1.5 convert_reduce_fusion.2
  57.1 1.5 convert_reduce_fusion.3
  58.7 4.6 %maximum_convert_fusion.8 = bf16[16,8,8,384]{3,0,2,1:T(8,128)(2,1)S(1)} fusion(bf16[3,3,448,384]{3,2,1,0:T(8,128)(2,1)S(1)} %copy-done, bf16[16,8,8,1152]{3,0,2,1:T(8,128)(2,1)S(1)} %fusion.5), kind=kOutput, calls=%fused_computation.22 | convolution fusion | flops 2665218048 | bytes 4931584 | tf_op jit(solution)/shard_map/conv_general_dilated | solution.py:19
  63.3 1.5 convert_reduce_fusion
  64.8 1.7 convert_reduce_fusion.1
  66.6 0.8 concatenate.7
  67.4 27.1 %all-gather.5.cloned.1.call-done = f32[128,2048]{1,0:T(8,128)} async-done(((f32[16,2048]{1,0:T(8,128)}), f32[128,2048]{1,0:T(8,128)}) %all-gather.5.cloned.1.call-update) | async-done | bytes 1048592 | tf_op jit(solution)/shard_map/all_gather | solution.py:135
  94.5 1.3 reduce_sum.69
  95.8 1.3 broadcast_subtract_fusion
  97.2 3.2 fusion.21
  101.0 0.8 dynamic-update-slice
  101.7 34.3 %all-reduce = f32[16]{0:T(128)S(1)} all-reduce(f32[16]{0:T(128)S(1)} %dynamic-update-slice), channel_id=1, replica_groups=mesh['sample'=16,'col'=8] {'sample'}, use_global_device_ids=true, to_apply=%add | all-reduce | flops 16 | bytes 128
  136.1 17.7 %all-gather = f32[32768]{0:T(1024)S(1)} all-gather(f32[2048]{0:T(1024)S(1)} %broadcast_multiply_fusion.6), channel_id=2, replica_groups=mesh['sample'=16,'col'=8] {'sample'}, dimensions={0}, use_global_device_ids=true | all-gather | bytes 139264 | tf_op jit(solution)/shard_map/all_gather | solution.py:8
  153.9 143.4 %all-gather.7.cloned.1.call-done = f32[32768,256]{1,0:T(8,128)} async-done(((f32[2048,256]{1,0:T(8,128)}), f32[32768,256]{1,0:T(8,128)}) %all-gather.7.cloned.1.call-update) | async-done | bytes 33554448 | tf_op jit(solution)/shard_map/all_gather | solution.py:8
  297.3 3.0 slice.31
  300.3 102.3 %while.21 = (s32[]{:T(128)}, f32[]{:T(128)}, f32[2048]{0:T(1024)S(1)}, f32[2048,256]{1,0:T(8,128)}, f32[16]{0:T(128)S(1)}, /*index=5*/f32[16,2048]{1,0:T(8,128)S...) while((s32[]{:T(128)}, f32[]{:T(128)}, f32[2048]{0:T(1024)S(1)}, ...), condition=%wide.region_10.11_spmd, body=%wide.region_9.0_spmd.sunk | while | flops 2103305 | bytes 6352095 | solution.py:13
  300.3 0.7 dynamic_slice.82
  303.2 3.9 fusion.47
  307.2 0.7 dynamic_slice.82
  310.1 3.9 fusion.47
  314.0 0.7 dynamic_slice.82
  316.9 3.9 fusion.47
  320.8 0.7 dynamic_slice.82
  323.7 3.9 fusion.47
  327.6 0.7 dynamic_slice.82
  330.5 3.9 fusion.47
  334.4 0.7 dynamic_slice.82
  337.4 3.9 fusion.47
  341.3 0.7 dynamic_slice.82
  344.2 3.9 fusion.47
  351.0 3.9 fusion.47
  357.8 3.9 fusion.47
  364.6 3.9 fusion.47
  371.5 3.9 fusion.47
  378.3 3.9 fusion.47
  385.1 3.9 fusion.47
  391.9 3.9 fusion.47
  398.7 3.9 fusion.47
  402.7 1.6 dynamic-slice_multiply_fusion
  (95 shorter events, 8.0 us)
Async XLA Ops:
  7.2 51.5 %copy-start = (bf16[3,3,448,384]{3,2,1,0:T(8,128)(2,1)S(1)}, bf16[3,3,448,384]{3,2,1,0:T(8,128)(2,1)}, u32[]{:S(2)}) copy-start(bf16[3,3,448,384]{3,2,1,0:T(8,128)(2,1)} %param.24) | copy-start | bytes 9289732
  7.2 87.4 %all-gather.5.cloned.1.call-start = ((), (), s32[]{:S(2)}) async-start(), calls=%async_computation | async-start | bytes 1179648 | tf_op jit(solution)/shard_map/all_gather | solution.py:135
  7.2 5.7 %copy-start.2 = (bf16[16,17,17,768]{3,0,2,1:T(8,128)(2,1)S(1)}, bf16[16,17,17,768]{3,0,2,1:T(8,128)(2,1)}, u32[]{:S(2)}) copy-start(bf16[16,17,17,768]{3,0,2,1:T(8,128)(2,1)} %param.15) | copy-start | bytes 21307396
  7.2 5.7 %copy-start.11 = (bf16[1,1,768,384]{3,2,1,0:T(8,128)(2,1)S(1)}, bf16[1,1,768,384]{3,2,1,0:T(8,128)(2,1)}, u32[]{:S(2)}) copy-start(bf16[1,1,768,384]{3,2,1,0:T(8,128)(2,1)} %param.16) | copy-start | bytes 1769476
  12.9 4.1 %copy-start.5 = (bf16[3,3,192,320]{3,2,1,0:T(8,128)(2,1)S(1)}, bf16[3,3,192,320]{3,2,1,0:T(8,128)(2,1)}, u32[]{:S(2)}) copy-start(bf16[3,3,192,320]{3,2,1,0:T(8,128)(2,1)} %param.17) | copy-start | bytes 3317764
  17.1 3.0 copy-start.10
  46.5 6.3 %copy-start.1 = (bf16[16,8,8,1280]{3,0,2,1:T(8,128)(2,1)S(1)}, bf16[16,8,8,1280]{3,0,2,1:T(8,128)(2,1)}, u32[]{:S(2)}) copy-start(bf16[16,8,8,1280]{3,0,2,1:T(8,128)(2,1)} %concatenate.6) | copy-start | bytes 7864324
  46.5 6.3 %copy-start.4 = (f32[8,8]{1,0:T(8,128)S(1)}, f32[8,8]{1,0:T(8,128)}, u32[]{:S(2)}) copy-start(f32[8,8]{1,0:T(8,128)} %constant.112.clone.1) | copy-start | bytes 772
  52.9 1.6 copy-start.12
  54.5 1.2 copy-start.6
  55.6 1.5 copy-start.7
  58.7 4.6 %copy-start.8 = (bf16[3,1,384,384]{3,2,1,0:T(8,128)(2,1)S(1)}, bf16[3,1,384,384]{3,2,1,0:T(8,128)(2,1)}, u32[]{:S(2)}) copy-start(bf16[3,1,384,384]{3,2,1,0:T(8,128)(2,1)} %param.26) | copy-start | bytes 2654212
  63.3 1.5 copy-start.9
  67.3 230.0 %all-gather.7.cloned.1.call-start = ((), (), s32[]{:S(2)}) async-start(), calls=%async_computation.1 | async-start | bytes 35651584 | tf_op jit(solution)/shard_map/all_gather | solution.py:8
  97.2 3.2 copy-start.13
  402.7 1.6 copy-start.3
Sparse Core Ops, SparseCore 0:
  67.5 27.0 all-gather.4
  100.5 196.7 all-gather.6
where the time goes:
time: 412 us; the launch traced here: 411 us
  waiting for transfers between devices  171 us (42%)
  other arithmetic  70.5 us (17%)
  blocking collectives  52.1 us (13%)
  matrix products  49.3 us (12%)
  loops' own time  32.1 us (8%)
  local copies, waits for them, and re-layouts  22.1 us (5%)
  between operations  14.4 us (3%)
    all_gather x1, waiting for transfers between devices, combined_all(): gathered = jax.tree.map(lambda a: lax.all_gather(a, axis), part)  143 us
    add x15, other arithmetic, combine(): moment_a + moment_b  58.7 us
    conv_general_dilated x11, matrix products, rectify(): lax.conv_general_dilated(inputs, kernel, (stride, stride), padding, dimen...  46.2 us
    unnamed x1, blocking collectives  34.3 us
    another operation x1, loops' own time, combined_all(): lax.fori_loop(1, lax.axis_size(axis), lambda source, state: combine(state...  32.1 us
    all_gather x1, waiting for transfers between devices, local(): gathered = lax.all_gather(features, 'col', axis=0, tiled=True)  27.1 us
    all_gather x1, blocking collectives, combined_all(): gathered = jax.tree.map(lambda a: lax.all_gather(a, axis), part)  17.7 us
    dynamic_slice x32, local copies, waits for them, and re-layouts, take(): lax.dynamic_index_in_dim(a, source, 0, False)  13.2 us
  transfers between devices with their start and end apart: 2, of which 2 were waited for; matrix products, arithmetic and copies ran while one was open for 0% of the time, Pallas kernels for 0%

commit v1 on v0

--- a/solution.py
+++ b/solution.py
@@ -132,7 +132,9 @@
         deep_column,
         pool_project,
     )
-    gathered = lax.all_gather(features, "col", axis=0, tiled=True)
+    gathered = jnp.concatenate(
+        lax.all_to_all(jnp.stack([features] * lax.axis_size("col")), "col", 0, 0), axis=0
+    )
     width = gathered.shape[1]
     col_width = width // lax.axis_size("col")
     col_start = lax.axis_index("col") * col_width

time: 412 us -> 407 us (0.988)
  waiting for transfers between devices: 171 us -> 158 us
  starting transfers between devices: 0.08 us -> 6.81 us
    all_gather x1 -> x0, waiting for transfers between devices: 27.1 us -> none  [local(): gathered = lax.all_gather(features, 'col', axis=0, tiled=True)]
    all_to_all x0 -> x1, waiting for transfers between devices: none -> 15.1 us  [local(): lax.all_to_all(jnp.stack([features] * lax.axis_size('col')), 'col', 0, 0)]
    all_to_all x0 -> x1, starting transfers between devices: none -> 6.81 us  [local(): lax.all_to_all(jnp.stack([features] * lax.axis_size('col')), 'col', 0, 0)]
where the time goes in v1:
time: 407 us; the launch traced here: 406 us
  waiting for transfers between devices  158 us (39%)
  other arithmetic  70.5 us (17%)
  blocking collectives  52.5 us (13%)
  matrix products  49.3 us (12%)
  loops' own time  32.1 us (8%)
  local copies, waits for them, and re-layouts  22.6 us (6%)
  between operations  14.4 us (4%)
  starting transfers between devices  6.81 us (2%)
    all_gather x1, waiting for transfers between devices, combined_all(): gathered = jax.tree.map(lambda a: lax.all_gather(a, axis), part)  143 us
    add x15, other arithmetic, combine(): moment_a + moment_b  58.7 us
    conv_general_dilated x11, matrix products, rectify(): lax.conv_general_dilated(inputs, kernel, (stride, stride), padding, dimen...  46.1 us
    unnamed x1, blocking collectives  35 us
    another operation x1, loops' own time, combined_all(): lax.fori_loop(1, lax.axis_size(axis), lambda source, state: combine(state...  32.1 us
    all_gather x1, blocking collectives, combined_all(): gathered = jax.tree.map(lambda a: lax.all_gather(a, axis), part)  17.6 us
    all_to_all x1, waiting for transfers between devices, local(): lax.all_to_all(jnp.stack([features] * lax.axis_size('col')), 'col', 0, 0)  15.1 us
    dynamic_slice x32, local copies, waits for them, and re-layouts, take(): lax.dynamic_index_in_dim(a, source, 0, False)  13.2 us
  transfers between devices with their start and end apart: 2, of which 2 were waited for; matrix products, arithmetic and copies ran while one was open for 0% of the time, Pallas kernels for 0%

profile of v1, /device:TPU:1, one launch (start us, length us, event | category | flops | bytes accessed | tf_op | source)
XLA Modules:
  0.0 406.5 jit_solution(2246159376834056518)
XLA Ops:
  7.2 5.7 %fusion.26 = bf16[16,8,8,768]{3,0,2,1:T(8,128)(2,1)} fusion(bf16[16,17,17,768]{3,0,2,1:T(8,128)(2,1)} %param.15), kind=kOutput, calls=%fused_computation.51 | output fusion | flops 6291456 | bytes 8675328 | tf_op jit(solution)/shard_map/reduce_window | solution.py:56
  12.9 4.1 %maximum_convert_fusion = bf16[16,17,17,384]{3,0,2,1:T(8,128)(2,1)S(1)} fusion(bf16[16,17,17,768]{3,0,2,1:T(8,128)(2,1)S(1)} %copy-done.2, bf16[1,1,768,384]{3,2,1,0:T(8,128)(2,1)S(1)} %copy-done.11), kind=kOutput, calls=%fused_computation.4 | convolution fusion | flops 2730897408 | bytes 11243520 | tf_op jit(solution)/shard_map/conv_general_dilated | solution.py:19
  17.0 3.0 maximum_convert_fusion.11
  20.0 11.7 %fusion.7 = bf16[16,17,17,192]{3,0,2,1:T(8,128)(2,1)} fusion(bf16[1,7,192,192]{3,2,1,0:T(8,128)(2,1)S(1)} %copy-done.10, bf16[16,17,17,384]{3,0,2,1:T(8,128)(2,1)S(1)} %maximum_convert_fusion), kind=kOutput, calls=%fused_computation.13 | convolution fusion | flops 2145779712 | bytes 4831232 | tf_op jit(solution)/shard_map/conv_general_dilated | solution.py:19
  31.7 9.4 %fusion.14 = bf16[16,8,8,192]{3,0,2,1:T(8,128)(2,1)} fusion(bf16[3,3,192,192]{3,2,1,0:T(8,128)(2,1)} %param.20, bf16[7,1,192,192]{3,2,1,0:T(8,128)(2,1)} %param.19, bf16[16,17,17,192]{3,0,2,1:T(8,128)(2,1)} %fusion.7), kind=kOutput, calls=%fused_computation.31 | convolution fusion | flops 2830089216 | bytes 3348480 | tf_op jit(solution)/shard_map/conv_general_dilated | solution.py:19
  41.1 5.4 %concatenate.6 = bf16[16,8,8,1280]{3,0,2,1:T(8,128)(2,1)} concatenate(bf16[16,8,8,320]{3,0,2,1:T(8,128)(2,1)} %maximum_convert_fusion.11, bf16[16,8,8,192]{3,0,2,1:T(8,128)(2,1)} %fusion.14, bf16[16,8,8,768]{3,0,2,1:T(8,128)(2,1)} %fusion.26), dimensions={3} | concatenate | bytes 5242880 | tf_op jit(solution)/shard_map/concatenate | solution.py:64
  46.5 6.3 %fusion.5 = bf16[16,8,8,1152]{3,0,2,1:T(8,128)(2,1)S(1)} fusion(bf16[16,8,8,1280]{3,0,2,1:T(8,128)(2,1)} %concatenate.6, bf16[1,1,1280,1152]{3,2,1,0:T(8,128)(2,1)} %param.21), kind=kOutput, calls=%fused_computation.11 | convolution fusion | flops 3022258176 | bytes 7929856 | tf_op jit(solution)/shard_map/conv_general_dilated | solution.py:19
  52.8 1.6 multiply_convert_fusion
  54.4 0.9 fusion.17
  55.6 1.5 convert_reduce_fusion.2
  57.1 1.5 convert_reduce_fusion.3
  58.7 4.6 %maximum_convert_fusion.8 = bf16[16,8,8,384]{3,0,2,1:T(8,128)(2,1)S(1)} fusion(bf16[3,3,448,384]{3,2,1,0:T(8,128)(2,1)S(1)} %copy-done, bf16[16,8,8,1152]{3,0,2,1:T(8,128)(2,1)S(1)} %fusion.5), kind=kOutput, calls=%fused_computation.22 | convolution fusion | flops 2665218048 | bytes 4931584 | tf_op jit(solution)/shard_map/conv_general_dilated | solution.py:19
  63.3 1.5 convert_reduce_fusion
  64.7 1.7 convert_reduce_fusion.1
  66.6 1.1 stack.2
  67.8 6.8 %all-to-all-start = ((f32[8,16,2048]{2,1,0:T(8,128)}), f32[8,16,2048]{2,1,0:T(8,128)}, u32[]{:S(2)}, u32[]{:S(2)}) async-start(f32[8,16,2048]{2,1,0:T(8,128)} %stack.2), calls=%async_computation | async-start | bytes 2097152 | tf_op jit(solution)/shard_map/all_to_all | solution.py:136
  74.6 15.1 %all-to-all-done = f32[8,16,2048]{2,1,0:T(8,128)} async-done(((f32[8,16,2048]{2,1,0:T(8,128)}), f32[8,16,2048]{2,1,0:T(8,128)}, u32[]{:S(2)}, u32[]{:S(2)}) %all-to-all-start) | async-done | bytes 1048608 | tf_op jit(solution)/shard_map/all_to_all | solution.py:136
  89.6 1.3 reduce_sum.69
  90.9 1.3 bitcast_subtract_fusion
  92.3 3.2 fusion.21
  96.1 0.8 dynamic-update-slice
  96.8 35.0 %all-reduce = f32[16]{0:T(128)S(1)} all-reduce(f32[16]{0:T(128)S(1)} %dynamic-update-slice), channel_id=1, replica_groups=mesh['sample'=16,'col'=8] {'sample'}, use_global_device_ids=true, to_apply=%add | all-reduce | flops 16 | bytes 128
  131.9 17.6 %all-gather = f32[32768]{0:T(1024)S(1)} all-gather(f32[2048]{0:T(1024)S(1)} %broadcast_multiply_fusion.6), channel_id=2, replica_groups=mesh['sample'=16,'col'=8] {'sample'}, dimensions={0}, use_global_device_ids=true | all-gather | bytes 139264 | tf_op jit(solution)/shard_map/all_gather | solution.py:8
  149.5 143.2 %all-gather.4.cloned.1.call-done = f32[32768,256]{1,0:T(8,128)} async-done(((f32[2048,256]{1,0:T(8,128)}), f32[32768,256]{1,0:T(8,128)}) %all-gather.4.cloned.1.call-update) | async-done | bytes 33554448 | tf_op jit(solution)/shard_map/all_gather | solution.py:8
  292.7 3.0 slice.31
  295.7 102.3 %while.21 = (s32[]{:T(128)}, f32[]{:T(128)}, f32[2048]{0:T(1024)S(1)}, f32[2048,256]{1,0:T(8,128)}, f32[16]{0:T(128)S(1)}, /*index=5*/f32[16,2048]{1,0:T(8,128)S...) while((s32[]{:T(128)}, f32[]{:T(128)}, f32[2048]{0:T(1024)S(1)}, ...), condition=%wide.region_10.11_spmd, body=%wide.region_9.0_spmd.sunk | while | flops 2103305 | bytes 6352095 | solution.py:13
  295.7 0.7 dynamic_slice.82
  298.6 3.9 fusion.47
  302.5 0.7 dynamic_slice.82
  305.4 3.9 fusion.47
  309.4 0.7 dynamic_slice.82
  312.3 3.9 fusion.47
  316.2 0.7 dynamic_slice.82
  319.1 3.9 fusion.47
  323.0 0.7 dynamic_slice.82
  325.9 3.9 fusion.47
  329.8 0.7 dynamic_slice.82
  332.7 3.9 fusion.47
  339.5 3.9 fusion.47
  346.4 3.9 fusion.47
  353.2 3.9 fusion.47
  360.0 3.9 fusion.47
  366.8 3.9 fusion.47
  373.7 3.9 fusion.47
  380.5 3.9 fusion.47
  387.3 3.9 fusion.47
  394.1 3.9 fusion.47
  398.0 1.6 dynamic-slice_multiply_fusion
  (95 shorter events, 8.7 us)
Async XLA Ops:
  7.2 51.5 %copy-start = (bf16[3,3,448,384]{3,2,1,0:T(8,128)(2,1)S(1)}, bf16[3,3,448,384]{3,2,1,0:T(8,128)(2,1)}, u32[]{:S(2)}) copy-start(bf16[3,3,448,384]{3,2,1,0:T(8,128)(2,1)} %param.24) | copy-start | bytes 9289732
  7.2 5.7 %copy-start.2 = (bf16[16,17,17,768]{3,0,2,1:T(8,128)(2,1)S(1)}, bf16[16,17,17,768]{3,0,2,1:T(8,128)(2,1)}, u32[]{:S(2)}) copy-start(bf16[16,17,17,768]{3,0,2,1:T(8,128)(2,1)} %param.15) | copy-start | bytes 21307396
  7.2 5.7 %copy-start.11 = (bf16[1,1,768,384]{3,2,1,0:T(8,128)(2,1)S(1)}, bf16[1,1,768,384]{3,2,1,0:T(8,128)(2,1)}, u32[]{:S(2)}) copy-start(bf16[1,1,768,384]{3,2,1,0:T(8,128)(2,1)} %param.16) | copy-start | bytes 1769476
  12.9 4.1 %copy-start.5 = (bf16[3,3,192,320]{3,2,1,0:T(8,128)(2,1)S(1)}, bf16[3,3,192,320]{3,2,1,0:T(8,128)(2,1)}, u32[]{:S(2)}) copy-start(bf16[3,3,192,320]{3,2,1,0:T(8,128)(2,1)} %param.17) | copy-start | bytes 3317764
  17.0 3.0 copy-start.10
  46.5 6.3 %copy-start.1 = (bf16[16,8,8,1280]{3,0,2,1:T(8,128)(2,1)S(1)}, bf16[16,8,8,1280]{3,0,2,1:T(8,128)(2,1)}, u32[]{:S(2)}) copy-start(bf16[16,8,8,1280]{3,0,2,1:T(8,128)(2,1)} %concatenate.6) | copy-start | bytes 7864324
  46.5 6.3 %copy-start.4 = (f32[8,8]{1,0:T(8,128)S(1)}, f32[8,8]{1,0:T(8,128)}, u32[]{:S(2)}) copy-start(f32[8,8]{1,0:T(8,128)} %constant.112.clone.1) | copy-start | bytes 772
  52.8 1.6 copy-start.12
  54.4 1.2 copy-start.6
  55.6 1.5 copy-start.7
  58.6 4.6 %copy-start.8 = (bf16[3,1,384,384]{3,2,1,0:T(8,128)(2,1)S(1)}, bf16[3,1,384,384]{3,2,1,0:T(8,128)(2,1)}, u32[]{:S(2)}) copy-start(bf16[3,1,384,384]{3,2,1,0:T(8,128)(2,1)} %param.26) | copy-start | bytes 2654212
  63.2 1.5 copy-start.9
  67.8 21.9 %all-to-all-start = ((f32[8,16,2048]{2,1,0:T(8,128)}), f32[8,16,2048]{2,1,0:T(8,128)}, u32[]{:S(2)}, u32[]{:S(2)}) async-start(f32[8,16,2048]{2,1,0:T(8,128)} %stack.2), calls=%async_computation | async-start | bytes 2097152 | tf_op jit(solution)/shard_map/all_to_all | solution.py:136
  74.6 218.1 %all-gather.4.cloned.1.call-start = ((), (), s32[]{:S(2)}) async-start(), calls=%async_computation.1 | async-start | bytes 35651584 | tf_op jit(solution)/shard_map/all_gather | solution.py:8
  92.3 3.2 copy-start.13
  398.0 1.6 copy-start.3
Sparse Core Ops, SparseCore 0:
  95.6 197.0 all-gather.3
